TPU v7x, 1024 devices: a whole 4x4x32 slice. The times are simulated.
1024 devices in a mesh: seq: 8 (over x, core), dp: 128 (over z, y).
Axes of the slice: x: 4, y: 4, z: 32, core: 2. Of those that a mesh axis runs over, the one named last changes fastest.
Arguments:
- layer_input: bfloat16 [128, 2048, 4096], P('dp', None, 'seq'), may hold values from -6 to 6
- query_proj: bfloat16 [128, 2048, 512], P('dp', 'seq'), may hold values from -6 to 6
- key_proj: bfloat16 [128, 2048, 128], P('dp', 'seq'), may hold values from -6 to 6
- value_proj: bfloat16 [128, 2048, 128], P('dp', 'seq'), may hold values from -6 to 6
- out_grad: bfloat16 [128, 2048, 512], P('dp', 'seq'), may hold values from -0.1875 to 0.1875
- block_pos: int32 [128, 16], P('dp'), may hold values from 0 to 15, each once within a row
- doc_ids: int32 [128, 16], P('dp'), may hold values from 0 to 7, never falling along the last dimension, each value on 1 to 4 neighbouring positions
Outputs:
- weight_grad: float32 [4096, 768], P(('seq', 'dp'))
Inputs may be any that keep to these rules, and one draw needn't show every extreme that they name: Each row is a permutation: storage block j of a sequence holds the tokens of position block block_pos[j] in order. `doc_ids`: along a row the document numbers never fall; each document covers 1 to 4 whole position blocks, and one covers exactly 4.
All inputs are finite; a program needn't handle non-finite values.
Results may differ from a plain program's by a relative error of at most 0.0062.
Values may be sent and summed in bfloat16 or wider, within the bound.
A program may use at most 32 MiB of HBM per device.

v0:
```python
import jax
import jax.numpy as jnp
from jax import lax
from jax.sharding import PartitionSpec as P

masked_fill = -1e30


def token_labels(pos_row, doc_row, length):
    blocks = pos_row.shape[0]
    block_span = length // blocks
    indices = jnp.arange(blocks, dtype=jnp.int32)
    block_doc = jnp.sum(
        jnp.where(pos_row[:, None] == indices[None, :], doc_row[None, :], 0), axis=1
    )
    offsets = jnp.arange(length, dtype=jnp.int32) % block_span
    token_pos = jnp.repeat(pos_row, block_span) * block_span + offsets
    token_doc = jnp.repeat(block_doc, block_span)
    return (token_pos, token_doc)


def block_terms(
    queries,
    grad_heads,
    key_rows,
    value_rows,
    query_pos,
    query_doc,
    key_pos,
    key_doc,
    scaling,
    block_span,
):
    tok_count, head_count, head_dim = queries.shape
    blocks = key_rows.shape[0] // block_span

    def block_parts(block_id):
        first = block_id * block_span
        key_block = lax.dynamic_slice_in_dim(key_rows, first, block_span)
        value_block = lax.dynamic_slice_in_dim(value_rows, first, block_span)
        block_doc = lax.dynamic_slice_in_dim(key_doc, first, block_span)
        block_pos = lax.dynamic_slice_in_dim(key_pos, first, block_span)
        live_mask = (query_doc[:, None] == block_doc[None, :]) & (
            query_pos[:, None] >= block_pos[None, :]
        )
        return (key_block, value_block, live_mask)

    def guarded(block_id, update, state_in):
        alive = jnp.any(block_parts(block_id)[2])
        return lax.cond(alive, update, lambda unchanged: unchanged, state_in)

    def block_scores(key_block, live_mask):
        scores = (
            jnp.einsum("ihc,jc->hij", queries, key_block, preferred_element_type=jnp.float32)
            * scaling
        )
        return jnp.where(live_mask[None], scores, masked_fill)

    def first_pass(block_id, state_in):

        def update(state_now):
            row_peak, row_total = state_now
            key_block, value_block, live_mask = block_parts(block_id)
            masked = block_scores(key_block, live_mask)
            new_peak = jnp.maximum(row_peak, jnp.max(masked, axis=2, keepdims=True))
            added = jnp.sum(
                jnp.where(live_mask[None], jnp.exp(masked - new_peak), 0.0), axis=2, keepdims=True
            )
            return (new_peak, row_total * jnp.exp(row_peak - new_peak) + added)

        return guarded(block_id, update, state_in)

    start_peak = jnp.full((head_count, tok_count, 1), masked_fill, jnp.float32)
    start_total = jnp.zeros((head_count, tok_count, 1), jnp.float32)
    row_peak, row_total = lax.fori_loop(0, blocks, first_pass, (start_peak, start_total))

    def block_probs(key_block, live_mask):
        masked = block_scores(key_block, live_mask)
        return jnp.where(live_mask[None], jnp.exp(masked - row_peak), 0.0) / row_total

    def second_pass(block_id, attended):

        def update(acc_now):
            key_block, value_block, live_mask = block_parts(block_id)
            probs_b = block_probs(key_block, live_mask).astype(jnp.bfloat16)
            return acc_now + jnp.einsum(
                "hij,jc->hic", probs_b, value_block, preferred_element_type=jnp.float32
            )

        return guarded(block_id, update, attended)

    attended = lax.fori_loop(
        0, blocks, second_pass, jnp.zeros((head_count, tok_count, head_dim), jnp.float32)
    )
    row_delta = jnp.sum(jnp.transpose(grad_heads.astype(jnp.float32), (1, 0, 2)) * attended, axis=2)

    def third_pass(block_id, state_in):

        def update(state_now):
            query_acc, key_part, value_part = state_now
            key_block, value_block, live_mask = block_parts(block_id)
            probs = block_probs(key_block, live_mask)
            probs_b = probs.astype(jnp.bfloat16)
            dprobs = jnp.einsum(
                "ihc,jc->hij", grad_heads, value_block, preferred_element_type=jnp.float32
            )
            dscores = (probs * (dprobs - row_delta[..., None])).astype(jnp.bfloat16)
            query_acc = query_acc + jnp.einsum(
                "hij,jc->ihc", dscores, key_block, preferred_element_type=jnp.float32
            )
            key_new = (
                jnp.einsum("hij,ihc->jc", dscores, queries, preferred_element_type=jnp.float32)
                * scaling
            )
            value_new = jnp.einsum(
                "hij,ihc->jc", probs_b, grad_heads, preferred_element_type=jnp.float32
            )
            first = block_id * block_span
            key_part = lax.dynamic_update_slice_in_dim(key_part, key_new, first, 0)
            value_part = lax.dynamic_update_slice_in_dim(value_part, value_new, first, 0)
            return (query_acc, key_part, value_part)

        return guarded(block_id, update, state_in)

    start_query = jnp.zeros((tok_count, head_count, head_dim), jnp.float32)
    start_keys = jnp.zeros(key_rows.shape, jnp.float32)
    start_values = jnp.zeros(value_rows.shape, jnp.float32)
    query_acc, key_part, value_part = lax.fori_loop(
        0, blocks, third_pass, (start_query, start_keys, start_values)
    )
    query_grad = (query_acc * scaling).astype(jnp.bfloat16).reshape(tok_count, -1)
    return (query_grad, key_part, value_part)


def body(layer_input, query_proj, key_proj, value_proj, out_grad, block_pos, doc_ids):
    shards = lax.axis_size("seq")
    my_index = lax.axis_index("seq")
    tok_count = query_proj.shape[1]
    head_dim = key_proj.shape[2]
    head_count = query_proj.shape[2] // head_dim
    length = tok_count * shards
    scaling = head_dim ** (-0.5)
    key_all, value_all = (
        lax.all_gather(key_proj, "seq", axis=1, tiled=True),
        lax.all_gather(value_proj, "seq", axis=1, tiled=True),
    )
    key_rows = key_all[0]
    value_rows = value_all[0]
    key_pos, key_doc = token_labels(block_pos[0], doc_ids[0], length)
    query_pos = lax.dynamic_slice_in_dim(key_pos, my_index * tok_count, tok_count)
    query_doc = lax.dynamic_slice_in_dim(key_doc, my_index * tok_count, tok_count)
    queries = query_proj[0].reshape(tok_count, head_count, head_dim)
    grad_heads = out_grad[0].reshape(tok_count, head_count, head_dim)
    block_span = length // block_pos.shape[1]
    query_grad, key_part, value_part = block_terms(
        queries,
        grad_heads,
        key_rows,
        value_rows,
        query_pos,
        query_doc,
        key_pos,
        key_doc,
        scaling,
        block_span,
    )
    kv_part = jnp.concatenate([key_part, value_part], axis=1)
    owned = lax.psum_scatter(kv_part, "seq", scatter_dimension=0, tiled=True).astype(jnp.bfloat16)
    local_rows = jnp.concatenate([query_grad, owned], axis=1)
    grad_rows = lax.all_gather(local_rows[None], "seq", axis=1, tiled=True)[0]
    feature_slab = layer_input[0]
    return lax.psum_scatter(
        lax.dot_general(
            feature_slab, grad_rows, (((0,), (0,)), ((), ())), preferred_element_type=jnp.float32
        ),
        "dp",
        scatter_dimension=0,
        tiled=True,
    )


def solution(mesh):
    placed = (
        P("dp", None, "seq"),
        P("dp", "seq", None),
        P("dp", "seq", None),
        P("dp", "seq", None),
        P("dp", "seq", None),
        P("dp", None),
        P("dp", None),
    )
    return jax.shard_map(
        body, mesh=mesh, in_specs=placed, out_specs=P(("seq", "dp"), None), check_vma=False
    )
```

profile of v0, /device:TPU:6, one launch (start us, length us, event | category | flops | bytes accessed | tf_op | source)
XLA Modules:
  0.0 815.0 jit_solution(5627087575014878747)
XLA Ops:
  8.5 23.3 %all_gather.9 = bf16[1,2048,128]{2,1,0:T(8,128)(2,1)S(1)} all-gather(bf16[1,256,128]{2,1,0:T(8,128)(2,1)} %param.21), channel_id=1, replica_groups=mesh['seq'=8,'dp'=128] {'seq'}, dimensions={1}, use_global_device_ids=true | all-gather | bytes 589824 | tf_op jit(solution)/shard_map/all_gather | solution.py:144
  31.8 1.1 copy.39
  33.1 30.0 %while.48 = (s32[]{:T(128)}, f32[4,256,1]{1,0,2:T(4,128)S(1)}, f32[4,256,1]{1,0,2:T(4,128)S(1)}, s32[256]{0:T(256)S(1)}, s32[2048]{0:T(1024)S(1)}, /*index=5*/s3...) while((s32[]{:T(128)}, f32[4,256,1]{1,0,2:T(4,128)S(1)}, ...), condition=%wide.region_7.8_spmd, body=%wide.region_1.7_spmd.sunk | while | flops 34572296 | bytes 1505635 | solution.py:75
  63.1 15.0 %all_gather.10 = bf16[1,2048,128]{2,1,0:T(8,128)(2,1)} all-gather(bf16[1,256,128]{2,1,0:T(8,128)(2,1)S(1)} %copy-done.2), channel_id=1, replica_groups=mesh['seq'=8,'dp'=128] {'seq'}, dimensions={1}, use_global_device_ids=true | all-gather | bytes 589824 | tf_op jit(solution)/shard_map/all_gather | solution.py:145
  78.2 29.1 %while.49 = (s32[]{:T(128)}, f32[4,256,128]{2,1,0:T(8,128)S(1)}, s32[256]{0:T(256)S(1)}, s32[2048]{0:T(1024)S(1)}, s32[256]{0:T(256)S(1)}, /*index=5*/s32[2048]{...) while((s32[]{:T(128)}, f32[4,256,128]{2,1,0:T(8,128)S(1)}, ...), condition=%wide.region_12.13_spmd, body=%wide.region_8.12_spmd.sunk | while | flops 68255752 | bytes 1461599 | solution.py:92
  82.7 1.6 conditional.7
  83.0 1.3 convolution_add_fusion
  99.6 1.6 conditional.7
  99.9 1.3 convolution_add_fusion
  102.7 1.6 conditional.7
  103.0 1.3 convolution_add_fusion
  108.4 1.1 copy.41
  109.6 1.1 fusion.57
  112.9 39.7 %while.50 = (s32[]{:T(128)}, f32[256,4,128]{0,2,1:T(8,128)S(1)}, f32[2048,128]{1,0:T(8,128)}, f32[2048,128]{1,0:T(8,128)}, s32[256]{0:T(256)S(1)}, /*index=5*/s3...) while((s32[]{:T(128)}, f32[256,4,128]{0,2,1:T(8,128)S(1)}, ...), condition=%wide.region_18.19_spmd, body=%wide.region_14.18_spmd.sunk | while | flops 169328640 | bytes 4774371 | solution.py:128
  117.5 5.1 conditional.8
  137.9 5.1 conditional.8
  144.5 5.1 conditional.8
  152.6 3.0 pad_maximum_fusion
  155.8 71.7 %reduce-scatter.3.cloned.1.call-done = f32[256,256]{1,0:T(8,128)} async-done(((f32[2048,256]{1,0:T(8,128)}), f32[256,256]{1,0:T(8,128)}) %reduce-scatter.3.cloned.1.call-update) | async-done | bytes 262160 | tf_op jit(solution)/shard_map/reduce_scatter | solution.py:168
  229.4 51.4 %all-gather.3.cloned.1.call-done = bf16[2048,768]{0,1:T(8,128)(2,1)} async-done(((bf16[256,768]{0,1:T(8,128)(2,1)}), bf16[2048,768]{0,1:T(8,128)(2,1)}) %all-gather.3.cloned.1.call-update) | async-done | bytes 3145744 | tf_op jit(solution)/shard_map/all_gather | solution.py:170
  280.8 4.8 fusion.54
  285.6 1.3 dynamic-slice
  287.6 519.0 %all-reduce.3.cloned.1.call-done = f32[512,768]{0,1:T(8,128)} async-done(((f32[512,768]{0,1:T(8,128)}), f32[512,768]{0,1:T(8,128)}) %all-reduce.3.cloned.1.call-update) | async-done | bytes 1572880
  806.6 1.2 constant_dynamic-slice_fusion
  (275 shorter events, 74.1 us)
Async XLA Ops:
  6.5 274.3 %copy-start = (bf16[1,2048,512]{2,1,0:T(8,128)(2,1)S(1)}, bf16[1,2048,512]{2,1,0:T(8,128)(2,1)}, u32[]{:S(2)}) copy-start(bf16[1,2048,512]{2,1,0:T(8,128)(2,1)} %param.19) | copy-start | bytes 6291460
  6.5 220.9 %reduce-scatter.3.cloned.1.call-start = ((), (), s32[]{:S(2)}) async-start(), calls=%async_computation.1 | async-start | bytes 2359296 | tf_op jit(solution)/shard_map/reduce_scatter | solution.py:168
  33.1 30.0 %copy-start.2 = (bf16[1,256,128]{2,1,0:T(8,128)(2,1)S(1)}, bf16[1,256,128]{2,1,0:T(8,128)(2,1)}, u32[]{:S(2)}) copy-start(bf16[1,256,128]{2,1,0:T(8,128)(2,1)} %param.22) | copy-start | bytes 196612
  107.3 2.1 copy-start.1
  155.7 125.1 %all-gather.3.cloned.1.call-start = ((), (), s32[]{:S(2)}) async-start(), calls=%async_computation.2 | async-start | bytes 3538944 | tf_op jit(solution)/shard_map/all_gather | solution.py:170
  229.3 577.2 %all-reduce.3.cloned.1.call-start = ((), (), s32[]{:S(2)}) async-start(), calls=%async_computation.3 | async-start | bytes 3145728
Sparse Core Ops, SparseCore 0:
  155.8 71.6 reduce-scatter.2
  230.1 50.5 all-gather.2
  285.7 520.7 all-reduce.2
where the time goes:
time: 816 us; the launch traced here: 815 us
  waiting for transfers between devices  642 us (79%)
  other arithmetic  47 us (6%)
  blocking collectives  38.4 us (5%)
  loops' own time  31.8 us (4%)
  matrix products  23.7 us (3%)
  local copies, waits for them, and re-layouts  18 us (2%)
  between operations  13.9 us (2%)
    unnamed x4, waiting for transfers between devices  519 us
    reduce_scatter x1, waiting for transfers between devices, body(): lax.psum_scatter(kv_part, 'seq', scatter_dimension=0, tiled=True)  71.7 us
    all_gather x1, waiting for transfers between devices, body(): grad_rows = lax.all_gather(local_rows[None], 'seq', axis=1, tiled=True)[0]  51.4 us
    reduce_or x48, other arithmetic, guarded(): alive = jnp.any(block_parts(block_id)[2])  38 us
    all_gather x1, blocking collectives, body(): lax.all_gather(key_proj, 'seq', axis=1, tiled=True)  23.3 us
  transfers between devices with their start and end apart: 3, of which 3 were waited for; matrix products, arithmetic and copies ran while one was open for 0% of the time, Pallas kernels for 0%

commit v1 on v0

v1 whole, which is shorter than its diff:
```python
import functools

import jax
import jax.numpy as jnp
from jax import lax
from jax.experimental import pallas as pl
from jax.experimental.pallas import tpu as pltpu
from jax.sharding import PartitionSpec as P

MESH = pl.DeviceIdType.MESH
F32 = jnp.float32
BF16 = jnp.bfloat16
FILL = -1e30
BLK = 128
HD = 128
NT = (((1,), (1,)), ((), ()))
NN = (((1,), (0,)), ((), ()))
TN = (((0,), (0,)), ((), ()))


def dot(a, b, dims):
    return lax.dot_general(a, b, dims, preferred_element_type=F32)


class Links:
    def __init__(self, send_sems, recv_sems):
        self.send_sems, self.recv_sems = send_sems, recv_sems
        self.count = 0
        self.sent = []

    def copy(self, src, dst, device):
        made = pltpu.make_async_remote_copy(
            src_ref=src,
            dst_ref=dst,
            send_sem=self.send_sems.at[self.count],
            recv_sem=self.recv_sems.at[self.count],
            device_id=device,
            device_id_type=MESH,
        )
        self.count += 1
        self.sent.append(made)
        return made


class Gather:
    def __init__(self, links, buf, ring):
        self.buf = buf
        here, left, right, far, dev_left, dev_right, dev_pair = ring
        cp = links.copy
        self.c = [
            cp(buf.at[here], buf.at[here], dev_right),
            cp(buf.at[here], buf.at[here], dev_left),
            cp(buf.at[here], buf.at[here], dev_pair),
            cp(buf.at[left, 0], buf.at[left, 0], dev_right),
            cp(buf.at[right, 1], buf.at[right, 1], dev_left),
            cp(buf.at[left], buf.at[left], dev_pair),
            cp(buf.at[right], buf.at[right], dev_pair),
            cp(buf.at[far, 0], buf.at[far, 0], dev_pair),
            cp(buf.at[far, 1], buf.at[far, 1], dev_pair),
        ]

    def begin(self):
        for k in (0, 1, 2):
            self.c[k].start()

    def relay(self):
        self.c[0].wait_recv()
        self.c[3].start()
        self.c[5].start()
        self.c[1].wait_recv()
        self.c[4].start()
        self.c[6].start()

    def last(self):
        self.c[3].wait_recv()
        self.c[7].start()
        self.c[4].wait_recv()
        self.c[8].start()

    def end(self):
        for k in (2, 5, 6, 7, 8):
            self.c[k].wait_recv()


class RingSum:
    def __init__(self, links, out, via, got, place, dev_left, dev_right):
        self.out, self.via, self.got = out, via, got
        self.place = place
        self.left, self.right = lax.rem(place + 3, 4), lax.rem(place + 1, 4)
        far = lax.rem(place + 2, 4)
        cp = links.copy
        self.c = [
            cp(out.at[far, 0], via.at[0], dev_right),
            cp(out.at[far, 1], via.at[1], dev_left),
            cp(out.at[self.right, 1], got.at[0, 1], dev_right),
            cp(out.at[self.left, 0], got.at[1, 0], dev_left),
            cp(out.at[self.right, 0], got.at[0, 0], dev_right),
            cp(out.at[self.left, 1], got.at[1, 1], dev_left),
        ]

    def begin(self):
        for k in range(4):
            self.c[k].start()

    def relay(self):
        for k, there in ((0, self.right), (1, self.left)):
            self.c[k].wait_recv()
            both = self.out[there, k].astype(F32) + self.via[k].astype(F32)
            self.out[there, k] = both.astype(BF16)
            self.c[4 + k].start()

    def end(self):
        for k in (2, 3, 4, 5):
            self.c[k].wait_recv()

    def arrived(self, half):
        return self.got[0, half].astype(F32) + self.got[1, half].astype(F32)


class LineSum:
    def __init__(self, links, out, got, place, device_of):
        self.got = got
        self.c = []
        for k in (1, 2, 3):
            there = lax.rem(place + k, 4)
            self.c.append(links.copy(out.at[there], got.at[k - 1], device_of(there)))

    def begin(self):
        for c in self.c:
            c.start()

    def end(self):
        for c in self.c:
            c.wait_recv()

    def arrived(self):
        return self.got[0].astype(F32) + self.got[1].astype(F32) + self.got[2].astype(F32)


def kernel(
    pos_ref, doc_ref, x_hbm, q_hbm, k_hbm, v_hbm, og_hbm, out_ref,
    kv, q_v, og_v, x_v, xt, g_q, g_kv, key_at, bias_at, slot_at,
    part, pair_out, pair_got, keep, sx_out, sx_via, sx_got,
    yq_out, yq_via, yq_got, yk_out, yk_via, yk_got,
    zq_own, zq_out, zq_got, zk_own, zk_out, zk_got,
    rows, piece, fwd_out, fwd_got, bwd_out, bwd_got,
    local_sems, send_sems, recv_sems,
):
    me, dp = lax.axis_index("seq"), lax.axis_index("dp")
    x, c = me // 2, me % 2
    z, y = dp // 4, dp % 4
    zh, zl = z // 4, z % 4

    def at_x(place, core):
        return lax.rem(place, 4) * 2 + core

    left, right, far, pair = at_x(x + 3, c), at_x(x + 1, c), at_x(x + 2, c), at_x(x, 1 - c)
    y_left = (me, z * 4 + lax.rem(y + 3, 4))
    y_right = (me, z * 4 + lax.rem(y + 1, 4))

    def near(place):
        return (me, (zh * 4 + place) * 4 + y)

    def group(place):
        return (me, (lax.rem(place, 8) * 4 + zl) * 4 + y)

    z_prev, z_next = group(zh + 7), group(zh + 1)

    loads = [
        pltpu.make_async_copy(k_hbm, kv.at[me, :, :, pl.ds(0, HD)], local_sems.at[0]),
        pltpu.make_async_copy(v_hbm, kv.at[me, :, :, pl.ds(HD, HD)], local_sems.at[1]),
        pltpu.make_async_copy(x_hbm, x_v, local_sems.at[2]),
        pltpu.make_async_copy(q_hbm, q_v, local_sems.at[3]),
        pltpu.make_async_copy(og_hbm, og_v, local_sems.at[4]),
    ]
    for load in loads:
        load.start()

    barrier = pltpu.get_barrier_semaphore()
    peers = [(left, dp), (right, dp), (pair, dp), y_left, y_right, z_prev, z_next]
    peers += [near(lax.rem(zl + k, 4)) for k in (1, 2, 3)]
    for peer in peers:
        pl.semaphore_signal(barrier, inc=1, device_id=peer, device_id_type=MESH)
    pl.semaphore_wait(barrier, len(peers))

    links = Links(send_sems, recv_sems)
    ring = (me, left, right, far, (left, dp), (right, dp), (pair, dp))
    gather_kv = Gather(links, kv, ring)
    loads[0].wait()
    loads[1].wait()
    gather_kv.begin()

    hits = []
    for q in range(2):
        mine = pos_ref[0, me * 2 + q]
        doc = doc_ref[0, mine]
        key_at[q * 4] = me * 2 + q
        bias_at[q * 4] = jnp.float32(0.0)
        for j in range(1, 4):
            want = jnp.maximum(mine - j, 0)
            live = jnp.logical_and(mine >= j, doc_ref[0, want] == doc)
            spot = jnp.int32(0)
            for s in range(16):
                spot = jnp.where(pos_ref[0, s] == want, jnp.int32(s), spot)
            key_at[q * 4 + j] = spot
            bias_at[q * 4 + j] = jnp.where(live, jnp.float32(0.0), jnp.float32(FILL))
            hits.append((q, q * 4 + j, jnp.where(live, spot, jnp.int32(-1))))
    for s in range(16):
        for q in range(2):
            slot = jnp.int32(8)
            for owner, number, spot in hits:
                if owner == q:
                    slot = jnp.where(spot == s, jnp.int32(number), slot)
            slot_at[q * 16 + s] = slot

    loads[2].wait()
    new = lax.broadcasted_iota(jnp.int32, (512, 512), 0)
    old = lax.broadcasted_iota(jnp.int32, (512, 512), 1)
    source = (new // 4 % 8) * 64 + (new // 32 % 4) * 16 + (new // 128) * 4 + new % 4
    one_hot = (old == source).astype(F32).astype(BF16)

    def flip(t, carry):
        at = pl.multiple_of(t * 256, 256)
        xt[:, pl.ds(at, 256)] = dot(one_hot, x_v[pl.ds(at, 256), :], NT).astype(BF16)
        return carry

    lax.fori_loop(0, 4, flip, 0)
    gather_kv.relay()
    lax.fori_loop(4, 8, flip, 0)
    gather_kv.last()
    part[...] = jnp.zeros_like(part)
    loads[3].wait()
    loads[4].wait()
    gather_kv.end()

    scaling = HD ** (-0.5)
    key_row = lax.broadcasted_iota(jnp.int32, (BLK, 2 * BLK), 0)
    query_col = lax.broadcasted_iota(jnp.int32, (BLK, 2 * BLK), 1) % BLK
    causal = key_row <= query_col

    def attend(step, carry):
        q, pair_of_heads = step // 2, step % 2
        cols = pl.ds(pl.multiple_of(pair_of_heads * 256, 256), 256)
        q_two, og_two = q_v[q, :, cols], og_v[q, :, cols]
        queries = jnp.concatenate([q_two[:, :HD], q_two[:, HD:]], axis=0)
        grads = jnp.concatenate([og_two[:, :HD], og_two[:, HD:]], axis=0)
        blocks = []
        for j in range(4):
            spot = key_at[q * 4 + j]
            blocks.append(kv[spot // 2, spot % 2])
        both = jnp.concatenate(blocks, axis=0)
        keys, values = both[:, :HD], both[:, HD:]
        scores = dot(keys, queries, NT) * scaling
        masked = [jnp.where(causal, scores[:BLK], FILL)]
        for j in range(1, 4):
            masked.append(scores[j * BLK : (j + 1) * BLK] + bias_at[q * 4 + j])
        scores = jnp.concatenate(masked, axis=0)
        peak = jnp.max(scores, axis=0, keepdims=True)
        weights = jnp.exp(scores - peak)
        probs = weights * (1.0 / jnp.sum(weights, axis=0, keepdims=True))
        probs_b = probs.astype(BF16)
        dprobs = dot(values, grads, NT)
        delta = jnp.sum(probs_b.astype(F32) * dprobs, axis=0, keepdims=True)
        dscores = (probs * (dprobs - delta)).astype(BF16)
        dq = (dot(dscores, keys, TN) * scaling).astype(BF16)
        g_q[me, q, :, cols] = jnp.concatenate([dq[:BLK], dq[BLK:]], axis=1)
        dk = dot(dscores, queries, NN) * scaling
        dv = dot(probs_b, grads, NN)
        for j in range(4):
            block = slice(j * BLK, (j + 1) * BLK)
            part[q * 4 + j, :, :HD] += dk[block]
            part[q * 4 + j, :, HD:] += dv[block]
        return carry

    lax.fori_loop(0, 4, attend, 0)

    def to_block(core, half, place):
        s = (place * 2 + core) * 2 + half
        return part[slot_at[s]] + part[slot_at[16 + s]]

    def for_pair(place, carry):
        for half in range(2):
            pair_out[place, half] = to_block(1 - c, half, place).astype(BF16)
        return carry

    lax.fori_loop(0, 4, for_pair, 0)
    gather_q = Gather(links, g_q, ring)
    gather_q.begin()
    pair_copy = links.copy(pair_out, pair_got, (pair, dp))
    pair_copy.start()

    def for_self(place, carry):
        for half in range(2):
            keep[place, half] = to_block(c, half, place)
        return carry

    lax.fori_loop(0, 4, for_self, 0)
    sum_x = RingSum(links, sx_out, sx_via, sx_got, x, (left, dp), (right, dp))
    pair_copy.wait_recv()

    def join(place, carry):
        for half in range(2):
            total = keep[place, half] + pair_got[place, half].astype(F32)
            keep[place, half] = total
            sx_out[place, half] = total.astype(BF16)
        return carry

    lax.fori_loop(0, 4, join, 0)
    sum_x.begin()
    gather_q.relay()
    sum_x.relay()
    gather_q.last()
    sum_x.end()
    for half in range(2):
        total = part[half * 4] + keep[x, half] + sum_x.arrived(half)
        g_kv[me, half] = total.astype(BF16)
    gather_g = Gather(links, g_kv, ring)
    gather_g.begin()
    gather_q.end()

    def weigh(g_ref, out, columns):
        def tile(t, carry):
            cols = pl.ds(pl.multiple_of(t * 256, 256), 256)
            grads = g_ref[:, :, :, cols].reshape(2048, 256)
            term = dot(xt[...], grads, NN).astype(BF16)
            for k in range(4):
                for half in range(2):
                    out[k, half, :, cols] = term[k * 128 + half * 64 : k * 128 + half * 64 + 64]
            return carry

        lax.fori_loop(0, columns // 256, tile, 0)

    weigh(g_q, yq_out, 512)
    sum_yq = RingSum(links, yq_out, yq_via, yq_got, y, y_left, y_right)
    sum_yq.begin()
    gather_g.relay()
    gather_g.last()
    sum_yq.relay()
    gather_g.end()
    weigh(g_kv, yk_out, 256)
    sum_yk = RingSum(links, yk_out, yk_via, yk_got, y, y_left, y_right)
    sum_yk.begin()

    def to_line(sums, own, out):
        for half in range(2):
            total = sums.out[y, half].astype(F32) + sums.arrived(half)
            for k in range(2):
                some = total[k * 32 : (k + 1) * 32]
                own[half * 2 + k] = some
                out[half * 2 + k] = some.astype(BF16)

    sum_yq.end()
    to_line(sum_yq, zq_own, zq_out)
    line_q = LineSum(links, zq_out, zq_got, zl, near)
    line_q.begin()
    sum_yk.relay()
    sum_yk.end()
    to_line(sum_yk, zk_own, zk_out)
    line_k = LineSum(links, zk_out, zk_got, zl, near)
    line_k.begin()
    line_q.end()
    rows[:, :512] = zq_own[zl] + line_q.arrived()
    line_k.end()
    rows[:, 512:] = zk_own[zl] + line_k.arrived()
    for k in range(8):
        piece[k] = rows[k * 4 : (k + 1) * 4, :]

    fwd = [links.copy(fwd_out.at[k], fwd_got.at[k], z_next) for k in range(4)]
    bwd = [links.copy(bwd_out.at[k], bwd_got.at[k], z_prev) for k in range(3)]
    for k in range(4):
        ahead = piece[lax.rem(zh + 4 - k, 8)]
        if k > 0:
            fwd[k - 1].wait_recv()
            ahead = ahead + fwd_got[k - 1]
        fwd_out[k] = ahead
        fwd[k].start()
        if k < 3:
            behind = piece[lax.rem(zh + 5 + k, 8)]
            if k > 0:
                bwd[k - 1].wait_recv()
                behind = behind + bwd_got[k - 1]
            bwd_out[k] = behind
            bwd[k].start()
    bwd[2].wait_recv()
    near_sum = piece[zh] + bwd_got[2]
    fwd[3].wait_recv()
    out_ref[...] = near_sum + fwd_got[3]
    for made in links.sent:
        made.wait_send()


def body(layer_input, query_proj, key_proj, value_proj, out_grad, block_pos, doc_ids):
    hbm = pl.BlockSpec(memory_space=pl.ANY)
    smem = pl.BlockSpec(memory_space=pltpu.SMEM)

    def ring_buffers(half_rows, columns):
        return [
            pltpu.VMEM((4, 2, half_rows, columns), BF16),
            pltpu.VMEM((2, half_rows, columns), BF16),
            pltpu.VMEM((2, 2, half_rows, columns), BF16),
        ]

    def line_buffers(columns):
        return [
            pltpu.VMEM((4, 32, columns), F32),
            pltpu.VMEM((4, 32, columns), BF16),
            pltpu.VMEM((3, 32, columns), BF16),
        ]

    copies = 3 * 9 + 1 + 3 * 6 + 2 * 3 + 7
    return pl.pallas_call(
        kernel,
        out_shape=jax.ShapeDtypeStruct((4, 768), F32),
        in_specs=[smem, smem, hbm, hbm, hbm, hbm, hbm],
        out_specs=pl.BlockSpec(memory_space=pltpu.VMEM),
        scratch_shapes=[
            pltpu.VMEM((8, 2, BLK, 256), BF16),
            pltpu.VMEM((2, BLK, 512), BF16),
            pltpu.VMEM((2, BLK, 512), BF16),
            pltpu.VMEM((2048, 512), BF16),
            pltpu.VMEM((512, 2048), BF16),
            pltpu.VMEM((8, 2, BLK, 512), BF16),
            pltpu.VMEM((8, 2, BLK, 256), BF16),
            pltpu.SMEM((8,), jnp.int32),
            pltpu.SMEM((8,), F32),
            pltpu.SMEM((32,), jnp.int32),
            pltpu.VMEM((9, BLK, 256), F32),
            pltpu.VMEM((4, 2, BLK, 256), BF16),
            pltpu.VMEM((4, 2, BLK, 256), BF16),
            pltpu.VMEM((4, 2, BLK, 256), F32),
            *ring_buffers(BLK, 256),
            *ring_buffers(64, 512),
            *ring_buffers(64, 256),
            *line_buffers(512),
            *line_buffers(256),
            pltpu.VMEM((32, 768), F32),
            pltpu.VMEM((8, 4, 768), F32),
            pltpu.VMEM((4, 4, 768), F32),
            pltpu.VMEM((4, 4, 768), F32),
            pltpu.VMEM((3, 4, 768), F32),
            pltpu.VMEM((3, 4, 768), F32),
            pltpu.SemaphoreType.DMA((5,)),
            pltpu.SemaphoreType.DMA((copies,)),
            pltpu.SemaphoreType.DMA((copies,)),
        ],
        compiler_params=pltpu.CompilerParams(
            collective_id=0, has_side_effects=True, vmem_limit_bytes=56 * 1024 * 1024
        ),
    )(
        block_pos,
        doc_ids,
        layer_input.reshape(2048, 512),
        query_proj.reshape(2, BLK, 512),
        key_proj.reshape(2, BLK, HD),
        value_proj.reshape(2, BLK, HD),
        out_grad.reshape(2, BLK, 512),
    )


def solution(mesh):
    placed = (
        P("dp", None, "seq"),
        P("dp", "seq", None),
        P("dp", "seq", None),
        P("dp", "seq", None),
        P("dp", "seq", None),
        P("dp", None),
        P("dp", None),
    )
    return jax.shard_map(
        body, mesh=mesh, in_specs=placed, out_specs=P(("seq", "dp"), None), check_vma=False
    )
```

time: 816 us -> 92.3 us (0.11)
  waiting for transfers between devices: 642 us -> 0 us
  Pallas kernels: 0 us -> 90.7 us
  other arithmetic: 47 us -> 0 us
  blocking collectives: 38.4 us -> 0 us
  loops' own time: 31.8 us -> 0 us
  matrix products: 23.7 us -> 0 us
  local copies, waits for them, and re-layouts: 18 us -> 1.31 us
  between operations: 13.9 us -> 0.01 us
    unnamed x4 -> x0, waiting for transfers between devices: 519 us -> none
    pallas_call x0 -> x1, Pallas kernels: none -> 90.7 us  [body(): pl.pallas_call(kernel, out_shape=jax.ShapeDtypeStruct((4, 768), F32), in_...]
    reduce_scatter x1 -> x0, waiting for transfers between devices: 71.7 us -> none  [body(): lax.psum_scatter(kv_part, 'seq', scatter_dimension=0, tiled=True)]
    all_gather x1 -> x0, waiting for transfers between devices: 51.4 us -> none  [body(): grad_rows = lax.all_gather(local_rows[None], 'seq', axis=1, tiled=True)[0]]
    all_gather x2 -> x0, blocking collectives: 38.4 us -> none  [the longest x1 23.3 us: body(): lax.all_gather(key_proj, 'seq', axis=1, tiled=True)]
    reduce_or x48 -> x0, other arithmetic: 38 us -> none  [guarded(): alive = jnp.any(block_parts(block_id)[2])]
    another operation x51 -> x0, loops' own time: 31.8 us -> none  [the longest x1 11.6 us: block_terms(): lax.fori_loop(0, blocks, first_pass, (start_peak, start_total))]
    dot_general x22 -> x0, matrix products: 23.7 us -> none  [the longest x1 4.81 us: body(): lax.dot_general(feature_slab, grad_rows, (((0,), (0,)), ((), ())), prefer...]
  transfers between devices with their start and end apart: 3 -> 0, of which waited for: 3 -> 0; matrix products, arithmetic and copies ran while one was open for 0% -> 0% of each run, Pallas kernels for 0% -> 0%
where the time goes in v1:
time: 92.3 us; the launch traced here: 92 us
  Pallas kernels  90.7 us (98%)
  local copies, waits for them, and re-layouts  1.31 us (1%)
    pallas_call x1, Pallas kernels, body(): pl.pallas_call(kernel, out_shape=jax.ShapeDtypeStruct((4, 768), F32), in_...  90.7 us

profile of v1, /device:TPU:6, one launch (start us, length us, event | category | flops | bytes accessed | tf_op | source)
XLA Modules:
  0.0 92.0 jit_solution(12053896810212590436)
XLA Ops:
  0.0 90.7 %shard_map.73 = f32[4,768]{1,0:T(4,128)} custom-call(s32[1,16]{1,0:T(1,128)} %pos_ref.1, s32[1,16]{1,0:T(1,128)} %doc_ref.1, bf16[2048,512]{1,0:T(8,128)(2,1)} %bitcast.5, bf16[2,128,512]{2,1,0:T(8,128)(2,1)} %bitcast.6, bf16[2,128,128]{2,1,0:T(8,128)(2,1)} %bitcast.8, bf16[2,128,128]{2,1,0:T(8,128)(2,1)} %bitcast.9, bf16[2,128,512]{2,1,0:T(8,128)(2,1)} %bitcast.7), custom_call_target="tpu_custom_call" | custom-call | tf_op jit(solution)/shard_map/pallas_call | solution.py:411
  90.7 1.3 %copy.9 = f32[4,768]{1,0:T(4,128)} copy(f32[4,768]{1,0:T(4,128)} %shard_map.73) | data formatting | bytes 24576

commit v2 on v1

--- a/solution.py
+++ b/solution.py
@@ -13,6 +13,7 @@
 FILL = -1e30
 BLK = 128
 HD = 128
+COPIES = 4 * 11 + 1 + 3 * 6 + 2 * 3 + 2 * 7
 NT = (((1,), (1,)), ((), ()))
 NN = (((1,), (0,)), ((), ()))
 TN = (((0,), (0,)), ((), ()))
@@ -43,42 +44,43 @@
 
 
 class Gather:
-    def __init__(self, links, buf, ring):
-        self.buf = buf
+    def __init__(self, links, whole, half, ring):
         here, left, right, far, dev_left, dev_right, dev_pair = ring
-        cp = links.copy
-        self.c = [
-            cp(buf.at[here], buf.at[here], dev_right),
-            cp(buf.at[here], buf.at[here], dev_left),
-            cp(buf.at[here], buf.at[here], dev_pair),
-            cp(buf.at[left, 0], buf.at[left, 0], dev_right),
-            cp(buf.at[right, 1], buf.at[right, 1], dev_left),
-            cp(buf.at[left], buf.at[left], dev_pair),
-            cp(buf.at[right], buf.at[right], dev_pair),
-            cp(buf.at[far, 0], buf.at[far, 0], dev_pair),
-            cp(buf.at[far, 1], buf.at[far, 1], dev_pair),
+        plan = [
+            (half(here, 0), dev_right),
+            (half(here, 1), dev_left),
+            (half(here, 1), dev_right),
+            (half(here, 0), dev_left),
+            (whole(here), dev_pair),
+            (half(left, 0), dev_right),
+            (half(right, 1), dev_left),
+            (whole(left), dev_pair),
+            (whole(right), dev_pair),
+            (half(far, 0), dev_pair),
+            (half(far, 1), dev_pair),
         ]
+        self.c = [links.copy(ref, ref, device) for ref, device in plan]
 
     def begin(self):
-        for k in (0, 1, 2):
+        for k in range(5):
             self.c[k].start()
 
+    def forward(self, arrives, leaves):
+        for k, m in zip(arrives, leaves):
+            self.c[k].wait_recv()
+            self.c[m].start()
+
     def relay(self):
-        self.c[0].wait_recv()
-        self.c[3].start()
-        self.c[5].start()
-        self.c[1].wait_recv()
-        self.c[4].start()
-        self.c[6].start()
+        self.forward((0, 1), (5, 6))
+
+    def share(self):
+        self.forward((2, 3), (7, 8))
 
     def last(self):
-        self.c[3].wait_recv()
-        self.c[7].start()
-        self.c[4].wait_recv()
-        self.c[8].start()
+        self.forward((5, 6), (9, 10))
 
     def end(self):
-        for k in (2, 5, 6, 7, 8):
+        for k in (4, 7, 8, 9, 10):
             self.c[k].wait_recv()
 
 
@@ -138,13 +140,13 @@
 
 
 def kernel(
-    pos_ref, doc_ref, x_hbm, q_hbm, k_hbm, v_hbm, og_hbm, out_ref,
-    kv, q_v, og_v, x_v, xt, g_q, g_kv, key_at, bias_at, slot_at,
+    pos_hbm, doc_hbm, x_hbm, q_hbm, k_hbm, v_hbm, og_hbm, out_ref,
+    pos_ref, doc_ref, kv, q_v, og_v, x_v, xt, g_q, g_kv, key_at, bias_at, slot_at,
     part, pair_out, pair_got, keep, sx_out, sx_via, sx_got,
     yq_out, yq_via, yq_got, yk_out, yk_via, yk_got,
     zq_own, zq_out, zq_got, zk_own, zk_out, zk_got,
-    rows, piece, fwd_out, fwd_got, bwd_out, bwd_got,
-    local_sems, send_sems, recv_sems,
+    fq_own, fq_out, fq_got, fk_own, fk_out, fk_got,
+    local_sems, known_sems, send_sems, recv_sems,
 ):
     me, dp = lax.axis_index("seq"), lax.axis_index("dp")
     x, c = me // 2, me % 2
@@ -164,7 +166,8 @@
     def group(place):
         return (me, (lax.rem(place, 8) * 4 + zl) * 4 + y)
 
-    z_prev, z_next = group(zh + 7), group(zh + 1)
+    def at_z(shift):
+        return (me, lax.rem(z + shift + 32, 32) * 4 + y)
 
     loads = [
         pltpu.make_async_copy(k_hbm, kv.at[me, :, :, pl.ds(0, HD)], local_sems.at[0]),
@@ -172,23 +175,38 @@
         pltpu.make_async_copy(x_hbm, x_v, local_sems.at[2]),
         pltpu.make_async_copy(q_hbm, q_v, local_sems.at[3]),
         pltpu.make_async_copy(og_hbm, og_v, local_sems.at[4]),
+        pltpu.make_async_copy(pos_hbm, pos_ref, local_sems.at[5]),
+        pltpu.make_async_copy(doc_hbm, doc_ref, local_sems.at[6]),
     ]
     for load in loads:
         load.start()
 
     barrier = pltpu.get_barrier_semaphore()
-    peers = [(left, dp), (right, dp), (pair, dp), y_left, y_right, z_prev, z_next]
-    peers += [near(lax.rem(zl + k, 4)) for k in (1, 2, 3)]
+    peers = [(left, dp), (right, dp), (pair, dp), y_left, y_right, at_z(-1), at_z(1)]
     for peer in peers:
         pl.semaphore_signal(barrier, inc=1, device_id=peer, device_id_type=MESH)
     pl.semaphore_wait(barrier, len(peers))
 
     links = Links(send_sems, recv_sems)
     ring = (me, left, right, far, (left, dp), (right, dp), (pair, dp))
-    gather_kv = Gather(links, kv, ring)
+    gather_kv = Gather(links, lambda d: kv.at[d], lambda d, h: kv.at[d, h], ring)
     loads[0].wait()
     loads[1].wait()
     gather_kv.begin()
+
+    def tell(r):
+        for side, way in enumerate((1, -1)):
+            pl.semaphore_signal(
+                known_sems.at[2 * r + side], inc=1, device_id=at_z(way * 2**r), device_id_type=MESH
+            )
+
+    def hear(r):
+        for side in range(2):
+            pl.semaphore_wait(known_sems.at[2 * r + side], 1)
+
+    tell(0)
+    loads[5].wait()
+    loads[6].wait()
 
     hits = []
     for q in range(2):
@@ -226,11 +244,16 @@
 
     lax.fori_loop(0, 4, flip, 0)
     gather_kv.relay()
+    hear(0)
+    tell(1)
+    gather_kv.share()
     lax.fori_loop(4, 8, flip, 0)
     gather_kv.last()
     part[...] = jnp.zeros_like(part)
     loads[3].wait()
     loads[4].wait()
+    hear(1)
+    tell(2)
     gather_kv.end()
 
     scaling = HD ** (-0.5)
@@ -272,7 +295,16 @@
             part[q * 4 + j, :, HD:] += dv[block]
         return carry
 
-    lax.fori_loop(0, 4, attend, 0)
+    def gather_queries(q):
+        def half(d, h):
+            return g_q.at[d, q, pl.ds(h * 64, 64)]
+
+        return Gather(links, lambda d: g_q.at[d, q], half, ring)
+
+    gather_a, gather_b = gather_queries(0), gather_queries(1)
+    lax.fori_loop(0, 2, attend, 0)
+    gather_a.begin()
+    lax.fori_loop(2, 4, attend, 0)
 
     def to_block(core, half, place):
         s = (place * 2 + core) * 2 + half
@@ -284,8 +316,6 @@
         return carry
 
     lax.fori_loop(0, 4, for_pair, 0)
-    gather_q = Gather(links, g_q, ring)
-    gather_q.begin()
     pair_copy = links.copy(pair_out, pair_got, (pair, dp))
     pair_copy.start()
 
@@ -296,6 +326,7 @@
 
     lax.fori_loop(0, 4, for_self, 0)
     sum_x = RingSum(links, sx_out, sx_via, sx_got, x, (left, dp), (right, dp))
+    gather_a.relay()
     pair_copy.wait_recv()
 
     def join(place, carry):
@@ -307,16 +338,24 @@
 
     lax.fori_loop(0, 4, join, 0)
     sum_x.begin()
-    gather_q.relay()
+    hear(2)
+    tell(3)
+    gather_a.share()
     sum_x.relay()
-    gather_q.last()
+    gather_b.begin()
+    gather_a.last()
     sum_x.end()
     for half in range(2):
         total = part[half * 4] + keep[x, half] + sum_x.arrived(half)
         g_kv[me, half] = total.astype(BF16)
-    gather_g = Gather(links, g_kv, ring)
+    gather_g = Gather(links, lambda d: g_kv.at[d], lambda d, h: g_kv.at[d, h], ring)
     gather_g.begin()
-    gather_q.end()
+    gather_a.end()
+    gather_b.relay()
+    gather_b.share()
+    gather_b.last()
+    gather_g.relay()
+    gather_b.end()
 
     def weigh(g_ref, out, columns):
         def tile(t, carry):
@@ -333,7 +372,7 @@
     weigh(g_q, yq_out, 512)
     sum_yq = RingSum(links, yq_out, yq_via, yq_got, y, y_left, y_right)
     sum_yq.begin()
-    gather_g.relay()
+    gather_g.share()
     gather_g.last()
     sum_yq.relay()
     gather_g.end()
@@ -358,40 +397,37 @@
     to_line(sum_yk, zk_own, zk_out)
     line_k = LineSum(links, zk_out, zk_got, zl, near)
     line_k.begin()
-    line_q.end()
-    rows[:, :512] = zq_own[zl] + line_q.arrived()
-    line_k.end()
-    rows[:, 512:] = zk_own[zl] + line_k.arrived()
-    for k in range(8):
-        piece[k] = rows[k * 4 : (k + 1) * 4, :]
-
-    fwd = [links.copy(fwd_out.at[k], fwd_got.at[k], z_next) for k in range(4)]
-    bwd = [links.copy(bwd_out.at[k], bwd_got.at[k], z_prev) for k in range(3)]
-    for k in range(4):
-        ahead = piece[lax.rem(zh + 4 - k, 8)]
-        if k > 0:
-            fwd[k - 1].wait_recv()
-            ahead = ahead + fwd_got[k - 1]
-        fwd_out[k] = ahead
-        fwd[k].start()
-        if k < 3:
-            behind = piece[lax.rem(zh + 5 + k, 8)]
-            if k > 0:
-                bwd[k - 1].wait_recv()
-                behind = behind + bwd_got[k - 1]
-            bwd_out[k] = behind
-            bwd[k].start()
-    bwd[2].wait_recv()
-    near_sum = piece[zh] + bwd_got[2]
-    fwd[3].wait_recv()
-    out_ref[...] = near_sum + fwd_got[3]
+    hear(3)
+    order = (4, 3, 5, 2, 6, 1, 7)
+
+    def to_far(own, line, far_own, far_out, far_got):
+        line.end()
+        total = own[zl] + line.arrived()
+        for k in range(8):
+            some = total[k * 4 : (k + 1) * 4]
+            far_own[k] = some
+            far_out[k] = some.astype(BF16)
+        sends = []
+        for n, shift in enumerate(order):
+            sends.append(links.copy(far_out.at[lax.rem(zh + shift, 8)], far_got.at[n], group(zh + shift)))
+            sends[-1].start()
+        return sends
+
+    far_q = to_far(zq_own, line_q, fq_own, fq_out, fq_got)
+    far_k = to_far(zk_own, line_k, fk_own, fk_out, fk_got)
+    for sends, own, got, cols in ((far_q, fq_own, fq_got, slice(0, 512)), (far_k, fk_own, fk_got, slice(512, 768))):
+        total = own[zh]
+        for n in reversed(range(7)):
+            sends[n].wait_recv()
+            total = total + got[n].astype(F32)
+        out_ref[:, cols] = total
     for made in links.sent:
         made.wait_send()
+    assert links.count == COPIES
 
 
 def body(layer_input, query_proj, key_proj, value_proj, out_grad, block_pos, doc_ids):
     hbm = pl.BlockSpec(memory_space=pl.ANY)
-    smem = pl.BlockSpec(memory_space=pltpu.SMEM)
 
     def ring_buffers(half_rows, columns):
         return [
@@ -407,13 +443,21 @@
             pltpu.VMEM((3, 32, columns), BF16),
         ]
 
-    copies = 3 * 9 + 1 + 3 * 6 + 2 * 3 + 7
+    def far_buffers(columns):
+        return [
+            pltpu.VMEM((8, 4, columns), F32),
+            pltpu.VMEM((8, 4, columns), BF16),
+            pltpu.VMEM((7, 4, columns), BF16),
+        ]
+
     return pl.pallas_call(
         kernel,
         out_shape=jax.ShapeDtypeStruct((4, 768), F32),
-        in_specs=[smem, smem, hbm, hbm, hbm, hbm, hbm],
+        in_specs=[hbm, hbm, hbm, hbm, hbm, hbm, hbm],
         out_specs=pl.BlockSpec(memory_space=pltpu.VMEM),
         scratch_shapes=[
+            pltpu.SMEM((1, 16), jnp.int32),
+            pltpu.SMEM((1, 16), jnp.int32),
             pltpu.VMEM((8, 2, BLK, 256), BF16),
             pltpu.VMEM((2, BLK, 512), BF16),
             pltpu.VMEM((2, BLK, 512), BF16),
@@ -433,15 +477,12 @@
             *ring_buffers(64, 256),
             *line_buffers(512),
             *line_buffers(256),
-            pltpu.VMEM((32, 768), F32),
-            pltpu.VMEM((8, 4, 768), F32),
-            pltpu.VMEM((4, 4, 768), F32),
-            pltpu.VMEM((4, 4, 768), F32),
-            pltpu.VMEM((3, 4, 768), F32),
-            pltpu.VMEM((3, 4, 768), F32),
-            pltpu.SemaphoreType.DMA((5,)),
-            pltpu.SemaphoreType.DMA((copies,)),
-            pltpu.SemaphoreType.DMA((copies,)),
+            *far_buffers(512),
+            *far_buffers(256),
+            pltpu.SemaphoreType.DMA((7,)),
+            pltpu.SemaphoreType.REGULAR((8,)),
+            pltpu.SemaphoreType.DMA((COPIES,)),
+            pltpu.SemaphoreType.DMA((COPIES,)),
         ],
         compiler_params=pltpu.CompilerParams(
             collective_id=0, has_side_effects=True, vmem_limit_bytes=56 * 1024 * 1024

time: 92.3 us -> 84.9 us (0.920)
  Pallas kernels: 90.7 us -> 83.4 us
    pallas_call x1, Pallas kernels: 90.7 us -> 83.4 us  [body(): pl.pallas_call(kernel, out_shape=jax.ShapeDtypeStruct((4, 768), F32), in_...]
where the time goes in v2:
time: 84.9 us; the launch traced here: 84.7 us
  Pallas kernels  83.4 us (98%)
  local copies, waits for them, and re-layouts  1.31 us (2%)
    pallas_call x1, Pallas kernels, body(): pl.pallas_call(kernel, out_shape=jax.ShapeDtypeStruct((4, 768), F32), in_...  83.4 us

profile of v2, /device:TPU:6, one launch (start us, length us, event | category | flops | bytes accessed | tf_op | source)
XLA Modules:
  0.0 84.7 jit_solution(4273829927432016029)
XLA Ops:
  0.0 83.4 %shard_map.73 = f32[4,768]{1,0:T(4,128)} custom-call(s32[1,16]{1,0:T(1,128)} %pos_hbm.1, s32[1,16]{1,0:T(1,128)} %doc_hbm.1, bf16[2048,512]{1,0:T(8,128)(2,1)} %bitcast.5, bf16[2,128,512]{2,1,0:T(8,128)(2,1)} %bitcast.6, bf16[2,128,128]{2,1,0:T(8,128)(2,1)} %bitcast.8, bf16[2,128,128]{2,1,0:T(8,128)(2,1)} %bitcast.9, bf16[2,128,512]{2,1,0:T(8,128)(2,1)} %bitcast.7), custom_call_target="tpu_custom_call" | custom-call | tf_op jit(solution)/shard_map/pallas_call | solution.py:453
  83.4 1.3 %copy.9 = f32[4,768]{1,0:T(4,128)} copy(f32[4,768]{1,0:T(4,128)} %shard_map.73) | data formatting | bytes 24576

commit v3 on v2

--- a/solution.py
+++ b/solution.py
@@ -13,7 +13,8 @@
 FILL = -1e30
 BLK = 128
 HD = 128
-COPIES = 4 * 11 + 1 + 3 * 6 + 2 * 3 + 2 * 7
+CHUNKS = 3
+COPIES = 4 * 7 + 5 + CHUNKS * (6 + 3 + 7)
 NT = (((1,), (1,)), ((), ()))
 NN = (((1,), (0,)), ((), ()))
 TN = (((0,), (0,)), ((), ()))
@@ -44,43 +45,42 @@
 
 
 class Gather:
-    def __init__(self, links, whole, half, ring):
-        here, left, right, far, dev_left, dev_right, dev_pair = ring
+    def __init__(self, links, block, ring):
+        me, mate, prev_same, prev_mate, far_same, dev_next, dev_pair = ring
         plan = [
-            (half(here, 0), dev_right),
-            (half(here, 1), dev_left),
-            (half(here, 1), dev_right),
-            (half(here, 0), dev_left),
-            (whole(here), dev_pair),
-            (half(left, 0), dev_right),
-            (half(right, 1), dev_left),
-            (whole(left), dev_pair),
-            (whole(right), dev_pair),
-            (half(far, 0), dev_pair),
-            (half(far, 1), dev_pair),
+            (me, dev_pair),
+            (me, dev_next),
+            (mate, dev_next),
+            (prev_same, dev_next),
+            (prev_same, dev_pair),
+            (prev_mate, dev_pair),
+            (far_same, dev_pair),
         ]
-        self.c = [links.copy(ref, ref, device) for ref, device in plan]
+        self.c = [links.copy(block(d), block(d), device) for d, device in plan]
 
     def begin(self):
-        for k in range(5):
-            self.c[k].start()
-
-    def forward(self, arrives, leaves):
-        for k, m in zip(arrives, leaves):
-            self.c[k].wait_recv()
-            self.c[m].start()
+        self.c[1].start()
+        self.c[0].start()
+
+    def mate(self):
+        self.c[0].wait_recv()
+        self.c[2].start()
 
     def relay(self):
-        self.forward((0, 1), (5, 6))
+        self.c[1].wait_recv()
+        self.c[3].start()
+        self.c[4].start()
 
     def share(self):
-        self.forward((2, 3), (7, 8))
+        self.c[2].wait_recv()
+        self.c[5].start()
 
     def last(self):
-        self.forward((5, 6), (9, 10))
+        self.c[3].wait_recv()
+        self.c[6].start()
 
     def end(self):
-        for k in (4, 7, 8, 9, 10):
+        for k in (4, 5, 6):
             self.c[k].wait_recv()
 
 
@@ -141,11 +141,9 @@
 
 def kernel(
     pos_hbm, doc_hbm, x_hbm, q_hbm, k_hbm, v_hbm, og_hbm, out_ref,
-    pos_ref, doc_ref, kv, q_v, og_v, x_v, xt, g_q, g_kv, key_at, bias_at, slot_at,
-    part, pair_out, pair_got, keep, sx_out, sx_via, sx_got,
-    yq_out, yq_via, yq_got, yk_out, yk_via, yk_got,
-    zq_own, zq_out, zq_got, zk_own, zk_out, zk_got,
-    fq_own, fq_out, fq_got, fk_own, fk_out, fk_got,
+    pos_ref, doc_ref, kv, q_v, og_v, x_v, xt, g, key_at, bias_at, slot_at,
+    part, pair_out, pair_got, keep, sx_out, sx_got,
+    y_out, y_via, y_got, z_own, z_out, z_got, f_own, f_out, f_got, early,
     local_sems, known_sems, send_sems, recv_sems,
 ):
     me, dp = lax.axis_index("seq"), lax.axis_index("dp")
@@ -157,6 +155,9 @@
         return lax.rem(place, 4) * 2 + core
 
     left, right, far, pair = at_x(x + 3, c), at_x(x + 1, c), at_x(x + 2, c), at_x(x, 1 - c)
+    step = 1 + 2 * c
+    next_x, prev_x = x + step, x + 4 - step
+    dev_next, dev_pair = (at_x(next_x, c), dp), (pair, dp)
     y_left = (me, z * 4 + lax.rem(y + 3, 4))
     y_right = (me, z * 4 + lax.rem(y + 1, 4))
 
@@ -188,8 +189,8 @@
     pl.semaphore_wait(barrier, len(peers))
 
     links = Links(send_sems, recv_sems)
-    ring = (me, left, right, far, (left, dp), (right, dp), (pair, dp))
-    gather_kv = Gather(links, lambda d: kv.at[d], lambda d, h: kv.at[d, h], ring)
+    ring = (me, pair, at_x(prev_x, c), at_x(prev_x, 1 - c), far, dev_next, dev_pair)
+    gather_kv = Gather(links, lambda d: kv.at[d], ring)
     loads[0].wait()
     loads[1].wait()
     gather_kv.begin()
@@ -231,6 +232,8 @@
                     slot = jnp.where(spot == s, jnp.int32(number), slot)
             slot_at[q * 16 + s] = slot
 
+    gather_kv.mate()
+
     loads[2].wait()
     new = lax.broadcasted_iota(jnp.int32, (512, 512), 0)
     old = lax.broadcasted_iota(jnp.int32, (512, 512), 1)
@@ -244,14 +247,14 @@
 
     lax.fori_loop(0, 4, flip, 0)
     gather_kv.relay()
+    lax.fori_loop(4, 8, flip, 0)
+    gather_kv.share()
     hear(0)
     tell(1)
-    gather_kv.share()
-    lax.fori_loop(4, 8, flip, 0)
-    gather_kv.last()
     part[...] = jnp.zeros_like(part)
     loads[3].wait()
     loads[4].wait()
+    gather_kv.last()
     hear(1)
     tell(2)
     gather_kv.end()
@@ -262,7 +265,7 @@
     causal = key_row <= query_col
 
     def attend(step, carry):
-        q, pair_of_heads = step // 2, step % 2
+        pair_of_heads, q = step // 2, step % 2
         cols = pl.ds(pl.multiple_of(pair_of_heads * 256, 256), 256)
         q_two, og_two = q_v[q, :, cols], og_v[q, :, cols]
         queries = jnp.concatenate([q_two[:, :HD], q_two[:, HD:]], axis=0)
@@ -286,7 +289,7 @@
         delta = jnp.sum(probs_b.astype(F32) * dprobs, axis=0, keepdims=True)
         dscores = (probs * (dprobs - delta)).astype(BF16)
         dq = (dot(dscores, keys, TN) * scaling).astype(BF16)
-        g_q[me, q, :, cols] = jnp.concatenate([dq[:BLK], dq[BLK:]], axis=1)
+        g[pair_of_heads, me, q] = jnp.concatenate([dq[:BLK], dq[BLK:]], axis=1)
         dk = dot(dscores, queries, NN) * scaling
         dv = dot(probs_b, grads, NN)
         for j in range(4):
@@ -295,132 +298,142 @@
             part[q * 4 + j, :, HD:] += dv[block]
         return carry
 
-    def gather_queries(q):
-        def half(d, h):
-            return g_q.at[d, q, pl.ds(h * 64, 64)]
-
-        return Gather(links, lambda d: g_q.at[d, q], half, ring)
-
-    gather_a, gather_b = gather_queries(0), gather_queries(1)
-    lax.fori_loop(0, 2, attend, 0)
+    gather_a, gather_b, gather_c = (Gather(links, lambda d, n=n: g.at[n, d], ring) for n in range(CHUNKS))
+    lax.fori_loop(0, 2, attend, 0, unroll=True)
     gather_a.begin()
-    lax.fori_loop(2, 4, attend, 0)
-
-    def to_block(core, half, place):
-        s = (place * 2 + core) * 2 + half
+    lax.fori_loop(2, 4, attend, 0, unroll=True)
+    gather_a.mate()
+
+    def roles(core):
+        ahead = x + 1 + 2 * core
+        return at_x(x + 2, core), at_x(ahead, 1 - core), at_x(ahead, core), at_x(x, core)
+
+    def to_block(device, half):
+        s = device * 2 + half
         return part[slot_at[s]] + part[slot_at[16 + s]]
 
-    def for_pair(place, carry):
+    for r, device in enumerate(roles(1 - c)):
         for half in range(2):
-            pair_out[place, half] = to_block(1 - c, half, place).astype(BF16)
-        return carry
-
-    lax.fori_loop(0, 4, for_pair, 0)
-    pair_copy = links.copy(pair_out, pair_got, (pair, dp))
+            pair_out[r, half] = to_block(device, half).astype(BF16)
+    pair_copy = links.copy(pair_out, pair_got, dev_pair)
     pair_copy.start()
-
-    def for_self(place, carry):
+    for r, device in enumerate(roles(c)):
         for half in range(2):
-            keep[place, half] = to_block(c, half, place)
-        return carry
-
-    lax.fori_loop(0, 4, for_self, 0)
-    sum_x = RingSum(links, sx_out, sx_via, sx_got, x, (left, dp), (right, dp))
-    gather_a.relay()
+            keep[r, half] = to_block(device, half)
+    sum_far = links.copy(sx_out.at[0], sx_got.at[0], dev_next)
+    sum_other = links.copy(sx_out.at[1], sx_got.at[1], dev_next)
+    sum_same = links.copy(sx_out.at[2], sx_got.at[2], dev_next)
+    sum_cross = links.copy(sx_got.at[1], sx_got.at[3], dev_pair)
     pair_copy.wait_recv()
-
-    def join(place, carry):
+    for r in range(4):
         for half in range(2):
-            total = keep[place, half] + pair_got[place, half].astype(F32)
-            keep[place, half] = total
-            sx_out[place, half] = total.astype(BF16)
-        return carry
-
-    lax.fori_loop(0, 4, join, 0)
-    sum_x.begin()
+            total = keep[r, half] + pair_got[r, half].astype(F32)
+            if r < 2:
+                sx_out[r, half] = total.astype(BF16)
+            else:
+                keep[r, half] = total
+        if r == 0:
+            sum_far.start()
+        if r == 1:
+            sum_other.start()
     hear(2)
     tell(3)
+    gather_a.relay()
+    sum_far.wait_recv()
+    for half in range(2):
+        sx_out[2, half] = (keep[2, half] + sx_got[0, half].astype(F32)).astype(BF16)
+    sum_same.start()
+    gather_b.begin()
     gather_a.share()
-    sum_x.relay()
-    gather_b.begin()
+    sum_other.wait_recv()
+    sum_cross.start()
+    gather_b.mate()
+    sum_same.wait_recv()
+    sum_cross.wait_recv()
+    for half in range(2):
+        moved = sx_got[2, half].astype(F32) + sx_got[3, half].astype(F32)
+        g[2, me, half] = (part[half * 4] + keep[3, half] + moved).astype(BF16)
+    gather_c.begin()
     gather_a.last()
-    sum_x.end()
-    for half in range(2):
-        total = part[half * 4] + keep[x, half] + sum_x.arrived(half)
-        g_kv[me, half] = total.astype(BF16)
-    gather_g = Gather(links, lambda d: g_kv.at[d], lambda d, h: g_kv.at[d, h], ring)
-    gather_g.begin()
-    gather_a.end()
-    gather_b.relay()
-    gather_b.share()
-    gather_b.last()
-    gather_g.relay()
-    gather_b.end()
-
-    def weigh(g_ref, out, columns):
-        def tile(t, carry):
-            cols = pl.ds(pl.multiple_of(t * 256, 256), 256)
-            grads = g_ref[:, :, :, cols].reshape(2048, 256)
-            term = dot(xt[...], grads, NN).astype(BF16)
-            for k in range(4):
-                for half in range(2):
-                    out[k, half, :, cols] = term[k * 128 + half * 64 : k * 128 + half * 64 + 64]
-            return carry
-
-        lax.fori_loop(0, columns // 256, tile, 0)
-
-    weigh(g_q, yq_out, 512)
-    sum_yq = RingSum(links, yq_out, yq_via, yq_got, y, y_left, y_right)
-    sum_yq.begin()
-    gather_g.share()
-    gather_g.last()
-    sum_yq.relay()
-    gather_g.end()
-    weigh(g_kv, yk_out, 256)
-    sum_yk = RingSum(links, yk_out, yk_via, yk_got, y, y_left, y_right)
-    sum_yk.begin()
-
-    def to_line(sums, own, out):
+
+    def product(n, devices):
+        total = None
+        for device in devices:
+            tokens = pl.ds(pl.multiple_of(device * 256, 256), 256)
+            term = dot(xt[:, tokens], g[n, device].reshape(256, 256), NN)
+            total = term if total is None else total + term
+        return total
+
+    def weigh(n, term=None):
+        if term is None:
+            term = dot(xt[...], g[n].reshape(2048, 256), NN)
+        term = term.astype(BF16)
+        for k in range(4):
+            for half in range(2):
+                at = k * 128 + half * 64
+                y_out[n, k, half] = term[at : at + 64]
+        sums = RingSum(links, y_out.at[n], y_via.at[n], y_got.at[n], y, y_left, y_right)
+        sums.begin()
+        return sums
+
+    def to_line(n, sums):
+        sums.end()
         for half in range(2):
-            total = sums.out[y, half].astype(F32) + sums.arrived(half)
+            total = y_out[n, y, half].astype(F32) + sums.arrived(half)
             for k in range(2):
                 some = total[k * 32 : (k + 1) * 32]
-                own[half * 2 + k] = some
-                out[half * 2 + k] = some.astype(BF16)
-
-    sum_yq.end()
-    to_line(sum_yq, zq_own, zq_out)
-    line_q = LineSum(links, zq_out, zq_got, zl, near)
-    line_q.begin()
-    sum_yk.relay()
-    sum_yk.end()
-    to_line(sum_yk, zk_own, zk_out)
-    line_k = LineSum(links, zk_out, zk_got, zl, near)
-    line_k.begin()
-    hear(3)
+                z_own[n, half * 2 + k] = some
+                z_out[n, half * 2 + k] = some.astype(BF16)
+        line = LineSum(links, z_out.at[n], z_got.at[n], zl, near)
+        line.begin()
+        return line
+
     order = (4, 3, 5, 2, 6, 1, 7)
 
-    def to_far(own, line, far_own, far_out, far_got):
+    def to_far(n, line):
         line.end()
-        total = own[zl] + line.arrived()
+        total = z_own[n, zl] + line.arrived()
         for k in range(8):
             some = total[k * 4 : (k + 1) * 4]
-            far_own[k] = some
-            far_out[k] = some.astype(BF16)
+            f_own[n, k] = some
+            f_out[n, k] = some.astype(BF16)
         sends = []
-        for n, shift in enumerate(order):
-            sends.append(links.copy(far_out.at[lax.rem(zh + shift, 8)], far_got.at[n], group(zh + shift)))
+        for i, shift in enumerate(order):
+            there = lax.rem(zh + shift, 8)
+            sends.append(links.copy(f_out.at[n, there], f_got.at[n, i], group(there)))
             sends[-1].start()
         return sends
 
-    far_q = to_far(zq_own, line_q, fq_own, fq_out, fq_got)
-    far_k = to_far(zk_own, line_k, fk_own, fk_out, fk_got)
-    for sends, own, got, cols in ((far_q, fq_own, fq_got, slice(0, 512)), (far_k, fk_own, fk_got, slice(512, 768))):
-        total = own[zh]
-        for n in reversed(range(7)):
-            sends[n].wait_recv()
-            total = total + got[n].astype(F32)
-        out_ref[:, cols] = total
+    gather_c.mate()
+    gather_b.relay()
+    gather_c.relay()
+    gather_a.end()
+    sum_a = weigh(0)
+    gather_b.share()
+    gather_c.share()
+    gather_b.last()
+    sum_a.relay()
+    early[...] = product(2, (me, pair, at_x(prev_x, c), at_x(prev_x, 1 - c)))
+    gather_c.last()
+    gather_b.end()
+    sum_b = weigh(1)
+    gather_c.end()
+    sum_c = weigh(2, early[...] + product(2, (at_x(next_x, c), at_x(next_x, 1 - c), far, at_x(x + 2, 1 - c))))
+    sum_b.relay()
+    sum_c.relay()
+    line_a = to_line(0, sum_a)
+    line_b = to_line(1, sum_b)
+    line_c = to_line(2, sum_c)
+    hear(3)
+    far_a = to_far(0, line_a)
+    far_b = to_far(1, line_b)
+    far_c = to_far(2, line_c)
+    for n, sends in enumerate((far_a, far_b, far_c)):
+        total = f_own[n, zh]
+        for i in reversed(range(7)):
+            sends[i].wait_recv()
+            total = total + f_got[n, i].astype(F32)
+        out_ref[:, n * 256 : (n + 1) * 256] = total
     for made in links.sent:
         made.wait_send()
     assert links.count == COPIES
@@ -428,27 +441,6 @@
 
 def body(layer_input, query_proj, key_proj, value_proj, out_grad, block_pos, doc_ids):
     hbm = pl.BlockSpec(memory_space=pl.ANY)
-
-    def ring_buffers(half_rows, columns):
-        return [
-            pltpu.VMEM((4, 2, half_rows, columns), BF16),
-            pltpu.VMEM((2, half_rows, columns), BF16),
-            pltpu.VMEM((2, 2, half_rows, columns), BF16),
-        ]
-
-    def line_buffers(columns):
-        return [
-            pltpu.VMEM((4, 32, columns), F32),
-            pltpu.VMEM((4, 32, columns), BF16),
-            pltpu.VMEM((3, 32, columns), BF16),
-        ]
-
-    def far_buffers(columns):
-        return [
-            pltpu.VMEM((8, 4, columns), F32),
-            pltpu.VMEM((8, 4, columns), BF16),
-            pltpu.VMEM((7, 4, columns), BF16),
-        ]
 
     return pl.pallas_call(
         kernel,
@@ -463,8 +455,7 @@
             pltpu.VMEM((2, BLK, 512), BF16),
             pltpu.VMEM((2048, 512), BF16),
             pltpu.VMEM((512, 2048), BF16),
-            pltpu.VMEM((8, 2, BLK, 512), BF16),
-            pltpu.VMEM((8, 2, BLK, 256), BF16),
+            pltpu.VMEM((CHUNKS, 8, 2, BLK, 256), BF16),
             pltpu.SMEM((8,), jnp.int32),
             pltpu.SMEM((8,), F32),
             pltpu.SMEM((32,), jnp.int32),
@@ -472,13 +463,18 @@
             pltpu.VMEM((4, 2, BLK, 256), BF16),
             pltpu.VMEM((4, 2, BLK, 256), BF16),
             pltpu.VMEM((4, 2, BLK, 256), F32),
-            *ring_buffers(BLK, 256),
-            *ring_buffers(64, 512),
-            *ring_buffers(64, 256),
-            *line_buffers(512),
-            *line_buffers(256),
-            *far_buffers(512),
-            *far_buffers(256),
+            pltpu.VMEM((3, 2, BLK, 256), BF16),
+            pltpu.VMEM((4, 2, BLK, 256), BF16),
+            pltpu.VMEM((CHUNKS, 4, 2, 64, 256), BF16),
+            pltpu.VMEM((CHUNKS, 2, 64, 256), BF16),
+            pltpu.VMEM((CHUNKS, 2, 2, 64, 256), BF16),
+            pltpu.VMEM((CHUNKS, 4, 32, 256), F32),
+            pltpu.VMEM((CHUNKS, 4, 32, 256), BF16),
+            pltpu.VMEM((CHUNKS, 3, 32, 256), BF16),
+            pltpu.VMEM((CHUNKS, 8, 4, 256), F32),
+            pltpu.VMEM((CHUNKS, 8, 4, 256), BF16),
+            pltpu.VMEM((CHUNKS, 7, 4, 256), BF16),
+            pltpu.VMEM((512, 256), F32),
             pltpu.SemaphoreType.DMA((7,)),
             pltpu.SemaphoreType.REGULAR((8,)),
             pltpu.SemaphoreType.DMA((COPIES,)),

time: 84.9 us -> 83.5 us (0.984)
  the two profiles are of different devices: /device:TPU:6 before, /device:TPU:64 now
where the time goes in v3:
time: 83.5 us; the launch traced here: 83.3 us
  Pallas kernels  82 us (98%)
  local copies, waits for them, and re-layouts  1.31 us (2%)
    pallas_call x1, Pallas kernels, body(): pl.pallas_call(kernel, out_shape=jax.ShapeDtypeStruct((4, 768), F32), in_...  82 us

profile of v3, /device:TPU:64, one launch (start us, length us, event | category | flops | bytes accessed | tf_op | source)
XLA Modules:
  0.0 83.3 jit_solution(3366091045527519211)
XLA Ops:
  0.0 82.0 %shard_map.73 = f32[4,768]{1,0:T(4,128)} custom-call(s32[1,16]{1,0:T(1,128)} %pos_hbm.1, s32[1,16]{1,0:T(1,128)} %doc_hbm.1, bf16[2048,512]{1,0:T(8,128)(2,1)} %bitcast.5, bf16[2,128,512]{2,1,0:T(8,128)(2,1)} %bitcast.6, bf16[2,128,128]{2,1,0:T(8,128)(2,1)} %bitcast.8, bf16[2,128,128]{2,1,0:T(8,128)(2,1)} %bitcast.9, bf16[2,128,512]{2,1,0:T(8,128)(2,1)} %bitcast.7), custom_call_target="tpu_custom_call" | custom-call | tf_op jit(solution)/shard_map/pallas_call | solution.py:445
  82.0 1.3 %copy.9 = f32[4,768]{1,0:T(4,128)} copy(f32[4,768]{1,0:T(4,128)} %shard_map.73) | data formatting | bytes 24576

commit v4 on v3

--- a/solution.py
+++ b/solution.py
@@ -14,7 +14,7 @@
 BLK = 128
 HD = 128
 CHUNKS = 3
-COPIES = 4 * 7 + 5 + CHUNKS * (6 + 3 + 7)
+COPIES = 5 * 7 + 5 + CHUNKS * (6 + 3 + 7)
 NT = (((1,), (1,)), ((), ()))
 NN = (((1,), (0,)), ((), ()))
 TN = (((0,), (0,)), ((), ()))
@@ -141,9 +141,9 @@
 
 def kernel(
     pos_hbm, doc_hbm, x_hbm, q_hbm, k_hbm, v_hbm, og_hbm, out_ref,
-    pos_ref, doc_ref, kv, q_v, og_v, x_v, xt, g, key_at, bias_at, slot_at,
+    pos_ref, doc_ref, k_all, v_all, q_v, og_v, x_v, xt, g, key_at, bias_at, slot_at,
     part, pair_out, pair_got, keep, sx_out, sx_got,
-    y_out, y_via, y_got, z_own, z_out, z_got, f_own, f_out, f_got, early,
+    y_out, y_via, y_got, z_own, z_out, z_got, f_own, f_out, f_got, early, probs_at,
     local_sems, known_sems, send_sems, recv_sems,
 ):
     me, dp = lax.axis_index("seq"), lax.axis_index("dp")
@@ -171,8 +171,8 @@
         return (me, lax.rem(z + shift + 32, 32) * 4 + y)
 
     loads = [
-        pltpu.make_async_copy(k_hbm, kv.at[me, :, :, pl.ds(0, HD)], local_sems.at[0]),
-        pltpu.make_async_copy(v_hbm, kv.at[me, :, :, pl.ds(HD, HD)], local_sems.at[1]),
+        pltpu.make_async_copy(k_hbm, k_all.at[me], local_sems.at[0]),
+        pltpu.make_async_copy(v_hbm, v_all.at[me], local_sems.at[1]),
         pltpu.make_async_copy(x_hbm, x_v, local_sems.at[2]),
         pltpu.make_async_copy(q_hbm, q_v, local_sems.at[3]),
         pltpu.make_async_copy(og_hbm, og_v, local_sems.at[4]),
@@ -190,10 +190,12 @@
 
     links = Links(send_sems, recv_sems)
     ring = (me, pair, at_x(prev_x, c), at_x(prev_x, 1 - c), far, dev_next, dev_pair)
-    gather_kv = Gather(links, lambda d: kv.at[d], ring)
+    gather_k = Gather(links, lambda d: k_all.at[d], ring)
+    gather_v = Gather(links, lambda d: v_all.at[d], ring)
     loads[0].wait()
+    gather_k.begin()
     loads[1].wait()
-    gather_kv.begin()
+    gather_v.begin()
 
     def tell(r):
         for side, way in enumerate((1, -1)):
@@ -232,7 +234,8 @@
                     slot = jnp.where(spot == s, jnp.int32(number), slot)
             slot_at[q * 16 + s] = slot
 
-    gather_kv.mate()
+    gather_k.mate()
+    gather_v.mate()
 
     loads[2].wait()
     new = lax.broadcasted_iota(jnp.int32, (512, 512), 0)
@@ -245,45 +248,59 @@
         xt[:, pl.ds(at, 256)] = dot(one_hot, x_v[pl.ds(at, 256), :], NT).astype(BF16)
         return carry
 
-    lax.fori_loop(0, 4, flip, 0)
-    gather_kv.relay()
-    lax.fori_loop(4, 8, flip, 0)
-    gather_kv.share()
+    lax.fori_loop(0, 2, flip, 0)
+    gather_k.relay()
+    gather_v.relay()
     hear(0)
     tell(1)
+    lax.fori_loop(2, 5, flip, 0)
+    gather_k.share()
+    gather_v.share()
+    lax.fori_loop(5, 7, flip, 0)
+    gather_k.last()
+    gather_v.last()
+    hear(1)
+    tell(2)
+    lax.fori_loop(7, 8, flip, 0)
     part[...] = jnp.zeros_like(part)
     loads[3].wait()
     loads[4].wait()
-    gather_kv.last()
-    hear(1)
-    tell(2)
-    gather_kv.end()
+    gather_k.end()
 
     scaling = HD ** (-0.5)
     key_row = lax.broadcasted_iota(jnp.int32, (BLK, 2 * BLK), 0)
     query_col = lax.broadcasted_iota(jnp.int32, (BLK, 2 * BLK), 1) % BLK
     causal = key_row <= query_col
 
-    def attend(step, carry):
-        pair_of_heads, q = step // 2, step % 2
+    def operands(number):
+        pair_of_heads, q = number // 2, number % 2
         cols = pl.ds(pl.multiple_of(pair_of_heads * 256, 256), 256)
-        q_two, og_two = q_v[q, :, cols], og_v[q, :, cols]
-        queries = jnp.concatenate([q_two[:, :HD], q_two[:, HD:]], axis=0)
-        grads = jnp.concatenate([og_two[:, :HD], og_two[:, HD:]], axis=0)
-        blocks = []
-        for j in range(4):
-            spot = key_at[q * 4 + j]
-            blocks.append(kv[spot // 2, spot % 2])
-        both = jnp.concatenate(blocks, axis=0)
-        keys, values = both[:, :HD], both[:, HD:]
-        scores = dot(keys, queries, NT) * scaling
+        return pair_of_heads, q, cols
+
+    def stacked(two):
+        return jnp.concatenate([two[:, :HD], two[:, HD:]], axis=0)
+
+    def four_blocks(ref, q):
+        spots = [key_at[q * 4 + j] for j in range(4)]
+        return jnp.concatenate([ref[spot // 2, spot % 2] for spot in spots], axis=0)
+
+    def weigh_keys(number, carry):
+        _, q, cols = operands(number)
+        scores = dot(four_blocks(k_all, q), stacked(q_v[q, :, cols]), NT) * scaling
         masked = [jnp.where(causal, scores[:BLK], FILL)]
         for j in range(1, 4):
             masked.append(scores[j * BLK : (j + 1) * BLK] + bias_at[q * 4 + j])
         scores = jnp.concatenate(masked, axis=0)
         peak = jnp.max(scores, axis=0, keepdims=True)
         weights = jnp.exp(scores - peak)
-        probs = weights * (1.0 / jnp.sum(weights, axis=0, keepdims=True))
+        probs_at[number] = weights * (1.0 / jnp.sum(weights, axis=0, keepdims=True))
+        return carry
+
+    def attend(number, carry):
+        pair_of_heads, q, cols = operands(number)
+        queries, grads = stacked(q_v[q, :, cols]), stacked(og_v[q, :, cols])
+        keys, values = four_blocks(k_all, q), four_blocks(v_all, q)
+        probs = probs_at[number]
         probs_b = probs.astype(BF16)
         dprobs = dot(values, grads, NT)
         delta = jnp.sum(probs_b.astype(F32) * dprobs, axis=0, keepdims=True)
@@ -299,6 +316,8 @@
         return carry
 
     gather_a, gather_b, gather_c = (Gather(links, lambda d, n=n: g.at[n, d], ring) for n in range(CHUNKS))
+    lax.fori_loop(0, 4, weigh_keys, 0, unroll=2)
+    gather_v.end()
     lax.fori_loop(0, 2, attend, 0, unroll=True)
     gather_a.begin()
     lax.fori_loop(2, 4, attend, 0, unroll=True)
@@ -406,9 +425,9 @@
 
     gather_c.mate()
     gather_b.relay()
-    gather_c.relay()
     gather_a.end()
     sum_a = weigh(0)
+    gather_c.relay()
     gather_b.share()
     gather_c.share()
     gather_b.last()
@@ -450,7 +469,8 @@
         scratch_shapes=[
             pltpu.SMEM((1, 16), jnp.int32),
             pltpu.SMEM((1, 16), jnp.int32),
-            pltpu.VMEM((8, 2, BLK, 256), BF16),
+            pltpu.VMEM((8, 2, BLK, HD), BF16),
+            pltpu.VMEM((8, 2, BLK, HD), BF16),
             pltpu.VMEM((2, BLK, 512), BF16),
             pltpu.VMEM((2, BLK, 512), BF16),
             pltpu.VMEM((2048, 512), BF16),
@@ -475,6 +495,7 @@
             pltpu.VMEM((CHUNKS, 8, 4, 256), BF16),
             pltpu.VMEM((CHUNKS, 7, 4, 256), BF16),
             pltpu.VMEM((512, 256), F32),
+            pltpu.VMEM((4, 512, 256), F32),
             pltpu.SemaphoreType.DMA((7,)),
             pltpu.SemaphoreType.REGULAR((8,)),
             pltpu.SemaphoreType.DMA((COPIES,)),

time: 83.5 us -> 80.4 us (0.963)
  the two profiles are of different devices: /device:TPU:64 before, /device:TPU:8 now
where the time goes in v4:
time: 80.4 us; the launch traced here: 80.2 us
  Pallas kernels  78.9 us (98%)
  local copies, waits for them, and re-layouts  1.31 us (2%)
    pallas_call x1, Pallas kernels, body(): pl.pallas_call(kernel, out_shape=jax.ShapeDtypeStruct((4, 768), F32), in_...  78.9 us

profile of v4, /device:TPU:8, one launch (start us, length us, event | category | flops | bytes accessed | tf_op | source)
XLA Modules:
  0.0 80.2 jit_solution(1939719926534759067)
XLA Ops:
  0.0 78.9 %shard_map.73 = f32[4,768]{1,0:T(4,128)} custom-call(s32[1,16]{1,0:T(1,128)} %pos_hbm.1, s32[1,16]{1,0:T(1,128)} %doc_hbm.1, bf16[2048,512]{1,0:T(8,128)(2,1)} %bitcast.5, bf16[2,128,512]{2,1,0:T(8,128)(2,1)} %bitcast.6, bf16[2,128,128]{2,1,0:T(8,128)(2,1)} %bitcast.8, bf16[2,128,128]{2,1,0:T(8,128)(2,1)} %bitcast.9, bf16[2,128,512]{2,1,0:T(8,128)(2,1)} %bitcast.7), custom_call_target="tpu_custom_call" | custom-call | tf_op jit(solution)/shard_map/pallas_call | solution.py:464
  78.9 1.3 %copy.9 = f32[4,768]{1,0:T(4,128)} copy(f32[4,768]{1,0:T(4,128)} %shard_map.73) | data formatting | bytes 24576

commit v5 on v4

--- a/solution.py
+++ b/solution.py
@@ -14,7 +14,7 @@
 BLK = 128
 HD = 128
 CHUNKS = 3
-COPIES = 5 * 7 + 5 + CHUNKS * (6 + 3 + 7)
+COPIES = 6 * 7 + 5 + CHUNKS * (6 + 3 + 7)
 NT = (((1,), (1,)), ((), ()))
 NN = (((1,), (0,)), ((), ()))
 TN = (((0,), (0,)), ((), ()))
@@ -315,7 +315,8 @@
             part[q * 4 + j, :, HD:] += dv[block]
         return carry
 
-    gather_a, gather_b, gather_c = (Gather(links, lambda d, n=n: g.at[n, d], ring) for n in range(CHUNKS))
+    gather_a, gather_b = (Gather(links, lambda d, n=n: g.at[n, d], ring) for n in range(2))
+    gather_c = [Gather(links, lambda d, h=h: g.at[2, d, h], ring) for h in range(2)]
     lax.fori_loop(0, 4, weigh_keys, 0, unroll=2)
     gather_v.end()
     lax.fori_loop(0, 2, attend, 0, unroll=True)
@@ -372,7 +373,8 @@
     for half in range(2):
         moved = sx_got[2, half].astype(F32) + sx_got[3, half].astype(F32)
         g[2, me, half] = (part[half * 4] + keep[3, half] + moved).astype(BF16)
-    gather_c.begin()
+    for some in gather_c:
+        some.begin()
     gather_a.last()
 
     def product(n, devices):
@@ -423,20 +425,25 @@
             sends[-1].start()
         return sends
 
-    gather_c.mate()
+    for some in gather_c:
+        some.mate()
     gather_b.relay()
     gather_a.end()
     sum_a = weigh(0)
-    gather_c.relay()
+    for some in gather_c:
+        some.relay()
     gather_b.share()
-    gather_c.share()
+    for some in gather_c:
+        some.share()
     gather_b.last()
     sum_a.relay()
     early[...] = product(2, (me, pair, at_x(prev_x, c), at_x(prev_x, 1 - c)))
-    gather_c.last()
+    for some in gather_c:
+        some.last()
     gather_b.end()
     sum_b = weigh(1)
-    gather_c.end()
+    for some in gather_c:
+        some.end()
     sum_c = weigh(2, early[...] + product(2, (at_x(next_x, c), at_x(next_x, 1 - c), far, at_x(x + 2, 1 - c))))
     sum_b.relay()
     sum_c.relay()

time: 80.4 us -> 80.4 us (level)
  the two profiles are of different devices: /device:TPU:8 before, /device:TPU:6 now
where the time goes in v5:
time: 80.4 us; the launch traced here: 78.9 us
  Pallas kernels  77.6 us (97%)
  local copies, waits for them, and re-layouts  1.31 us (2%)
    pallas_call x1, Pallas kernels, body(): pl.pallas_call(kernel, out_shape=jax.ShapeDtypeStruct((4, 768), F32), in_...  77.6 us

profile of v5, /device:TPU:6, one launch (start us, length us, event | category | flops | bytes accessed | tf_op | source)
XLA Modules:
  0.0 78.9 jit_solution(6299054600836685512)
XLA Ops:
  0.0 77.6 %shard_map.73 = f32[4,768]{1,0:T(4,128)} custom-call(s32[1,16]{1,0:T(1,128)} %pos_hbm.1, s32[1,16]{1,0:T(1,128)} %doc_hbm.1, bf16[2048,512]{1,0:T(8,128)(2,1)} %bitcast.5, bf16[2,128,512]{2,1,0:T(8,128)(2,1)} %bitcast.6, bf16[2,128,128]{2,1,0:T(8,128)(2,1)} %bitcast.8, bf16[2,128,128]{2,1,0:T(8,128)(2,1)} %bitcast.9, bf16[2,128,512]{2,1,0:T(8,128)(2,1)} %bitcast.7), custom_call_target="tpu_custom_call" | custom-call | tf_op jit(solution)/shard_map/pallas_call | solution.py:471
  77.6 1.3 %copy.9 = f32[4,768]{1,0:T(4,128)} copy(f32[4,768]{1,0:T(4,128)} %shard_map.73) | data formatting | bytes 24576
